TPU v7x, 128 devices: a whole 4x4x4 slice. The times are simulated.
128 devices in a mesh: seq: 16 (over x, y_hi, core), fsdp: 8 (over z, y_lo).
Axes of the slice: x: 4, y: 4 (y_hi: 2, y_lo: 2; y = y_hi * 2 + y_lo), z: 4, core: 2. Of those that a mesh axis runs over, the one named last changes fastest.
Arguments:
- normed: bfloat16 [131072, 1024], P(('seq', 'fsdp')), may hold values from -31 to 31, as said below
- w_qkv: bfloat16 [1024, 3072], P('fsdp'), may hold values from -0.5 to 0.5, as said below
- w_out: bfloat16 [1024, 1024], P('fsdp'), may hold values from -0.5 to 0.5
- layout: int32 [1024, 10], P(('seq', 'fsdp')), may hold values from 0 to 23, as said below
- counts: int32 [1024], P(('seq', 'fsdp')), may hold values from 1 to 10, as said below
Outputs:
- mixed: bfloat16 [131072, 1024], P(('seq', 'fsdp'))
Inputs may be any that keep to these rules, and one draw needn't show every extreme that they name: `normed`: float activations. `w_qkv`: float weights. `layout`: each row holds 10 distinct pool entries, never the query block's own entry; entries 0 to 7 name the blocks of the station one step lower along seq, the last 8 those one step higher. `counts`: the value 10 occurs in every draw.
All inputs are finite; a program needn't handle non-finite values.
Results may differ from a plain program's by a relative error of at most 0.0099.
Values may be sent and summed in bfloat16 or wider, within the bound.
A program may use at most 128 MiB of HBM per device.

v0:
```python
import math
import jax
import jax.numpy as jnp
from jax import lax
from jax.sharding import PartitionSpec as P

HEADS = 8
BLOCK = 128
KEY_BLOCKS = 10


def from_behind(value, axis, steps):
    count = lax.axis_size(axis)
    pairs = [(source, (source + steps) % count) for source in range(count)]
    return lax.ppermute(value, axis, pairs)


def attend(query, own_blocks, picked, used):
    block_count = picked.shape[0]
    feature_width = query.shape[1]
    head_width = feature_width // HEADS
    keyvals = jnp.concatenate([own_blocks[:, None], picked], axis=1)
    keyvals = keyvals.reshape(block_count, (KEY_BLOCKS + 1) * BLOCK, 2 * feature_width)
    key_heads = keyvals[..., :feature_width].reshape(block_count, -1, HEADS, head_width)
    value_heads = keyvals[..., feature_width:].reshape(block_count, -1, HEADS, head_width)
    query_heads = query.reshape(block_count, BLOCK, HEADS, head_width)
    scores = jnp.einsum(
        "bqhd,bkhd->bhqk", query_heads, key_heads, preferred_element_type=jnp.float32
    )
    scores = scores * head_width ** (-0.5)
    slot_number = jnp.arange((KEY_BLOCKS + 1) * BLOCK, dtype=jnp.int32) // BLOCK
    usable = slot_number[None, :] <= used[:, None]
    scores = jnp.where(usable[:, None, None, :], scores, -jnp.inf)
    largest = jnp.max(scores, axis=-1, keepdims=True)
    expons = jnp.exp(scores - largest)
    denominator = jnp.sum(expons, axis=-1, keepdims=True)
    rounded = expons.astype(jnp.bfloat16)
    summed = jnp.einsum("bhqk,bkhd->bqhd", rounded, value_heads, preferred_element_type=jnp.float32)
    summed = summed / jnp.transpose(denominator, (0, 2, 1, 3))
    return summed.reshape(block_count * BLOCK, feature_width).astype(jnp.bfloat16)


def shards(normed, w_qkv, w_out, layout, counts):
    row_count, feature_width = normed.shape
    blocks_here = row_count // BLOCK
    sources = (normed,)
    start_sums = [jnp.zeros((row_count, 3 * feature_width), jnp.float32)]
    start_sums = tuple(start_sums)
    own_cols = sources[0]
    fresh = [
        jnp.dot(
            own_cols,
            lax.all_gather(w_qkv, "fsdp", axis=0, tiled=True),
            preferred_element_type=jnp.float32,
        )
    ]
    sums = tuple(fresh)
    packed = sums[0].astype(jnp.bfloat16)
    queries = packed[:, :feature_width]
    keyvals = packed[:, feature_width:]
    lower_keys = from_behind(keyvals, "seq", 1)
    upper_keys = from_behind(keyvals, "seq", -1)
    pool_rows = jnp.concatenate([lower_keys, keyvals, upper_keys], axis=0)
    pool = pool_rows.reshape(3 * blocks_here, BLOCK, 2 * feature_width)
    group_size = math.gcd(blocks_here, max(1, 256 // BLOCK))
    group_count = blocks_here // group_size

    def one_group(items):
        query_part, layout_part, count_part, group_number = items
        own_blocks = lax.dynamic_slice_in_dim(
            pool, blocks_here + group_number * group_size, group_size, 0
        )
        picked = pool[layout_part]
        return attend(query_part, own_blocks, picked, count_part)

    attended = lax.map(
        one_group,
        (
            queries.reshape(group_count, group_size * BLOCK, feature_width),
            layout.reshape(group_count, group_size, KEY_BLOCKS),
            counts.reshape(group_count, group_size),
            jnp.arange(group_count, dtype=jnp.int32),
        ),
    )
    attended = attended.reshape(row_count, feature_width)
    output_sum = jnp.dot(
        attended,
        lax.all_gather(w_out, "fsdp", axis=0, tiled=True),
        preferred_element_type=jnp.float32,
    )
    return output_sum.astype(jnp.bfloat16)


def solution(mesh):
    return jax.shard_map(
        shards,
        mesh=mesh,
        in_specs=(
            P(("seq", "fsdp"), None),
            P("fsdp", None),
            P("fsdp", None),
            P(("seq", "fsdp"), None),
            P(("seq", "fsdp")),
        ),
        out_specs=P(("seq", "fsdp"), None),
        check_vma=False,
    )
```

profile of v0, /device:TPU:1, one launch (start us, length us, event | category | flops | bytes accessed | tf_op | source)
XLA Modules:
  0.0 604.0 jit_solution(1905112295235655145)
XLA Ops:
  6.5 0.7 all-gather.3.cloned.1.call-update
  7.3 134.3 %all-gather.3.cloned.1.call-done = bf16[1024,3072]{1,0:T(8,128)(2,1)} async-done(((bf16[128,3072]{1,0:T(8,128)(2,1)}), bf16[1024,3072]{1,0:T(8,128)(2,1)}) %all-gather.3.cloned.1.call-update) | async-done | bytes 6291472 | tf_op jit(solution)/shard_map/all_gather | solution.py:53
  141.6 9.6 %convolution_convert_fusion = bf16[1024,3072]{1,0:T(8,128)(2,1)S(1)} fusion(bf16[1024,1024]{1,0:T(8,128)(2,1)S(1)} %copy-done, bf16[1024,3072]{1,0:T(8,128)(2,1)} %all-gather.3.cloned.1.call-done), kind=kOutput, calls=%fused_computation.36 | convolution fusion | flops 6445596672 | bytes 14680064 | tf_op jit(solution)/shard_map/dot_general | solution.py:51
  151.3 2.7 copy-done.3
  153.9 2.2 slice.24
  156.2 3.2 collective-permute-start
  159.5 3.1 slice.25
  162.6 126.8 %collective-permute-done = bf16[1024,2048]{1,0:T(8,128)(2,1)} collective-permute-done((bf16[1024,2048]{1,0:T(8,128)(2,1)}, bf16[1024,2048]{1,0:T(8,128)(2,1)}, u32[]{:S(2)}, u32[]{:S(2)}) %collective-permute-start) | collective-permute-done | bytes 4194336 | tf_op jit(solution)/shard_map/ppermute | solution.py:15
  289.4 3.1 collective-permute-done.1
  292.5 11.4 %pad_maximum_fusion.1 = bf16[3072,2048]{1,0:T(8,128)(2,1)} fusion(bf16[1024,2048]{1,0:T(8,128)(2,1)} %collective-permute-done.1, bf16[1024,2048]{1,0:T(8,128)(2,1)} %slice.24, bf16[1024,2048]{1,0:T(8,128)(2,1)} %collective-permute-done), kind=kLoop, calls=%fused_computation.35 | loop fusion | flops 37748736 | bytes 25165824 | tf_op jit(solution)/shard_map/concatenate | solution.py:63
  303.9 287.3 %while.12 = (s32[]{:T(128)}, bf16[4,256,1024]{2,1,0:T(8,128)(2,1)}, s32[4]{0:T(128)S(1)}, bf16[24,128,2048]{2,1,0:T(8,128)(2,1)}, s32[4,2,10]{2,1,0:T(2,128)}, /...) while((s32[]{:T(128)}, bf16[4,256,1024]{2,1,0:T(8,128)(2,1)}, ...), condition=%wide.region_3.4_spmd, body=%wide.region_0.3_spmd.sunk | while | flops 1514416896 | bytes 190909680 | solution.py:76
  305.0 1.3 dynamic-slice_bitcast_fusion.4
  306.3 0.7 compare_select_fusion.2
  307.1 10.0 %gather_fusion = bf16[20,128,2048]{2,1,0:T(8,128)(2,1)} fusion(bf16[24,128,2048]{2,1,0:T(8,128)(2,1)} %get-tuple-element.200, s32[1024]{0:T(1024)S(1)} %pad_clamp_fusion.2), kind=kCustom, calls=%fused_computation.clone.1 | custom fusion | bytes 20971600 | tf_op jit(solution)/shard_map/while/body/eval_jaxpr/gather | solution.py:73
  317.1 10.1 %pad_maximum_fusion.3 = bf16[2,11,128,2048]{3,2,1,0:T(8,128)(2,1)} fusion(bf16[2,10,128,2048]{3,2,1,0:T(8,128)(2,1)} %bitcast.74, bf16[2,1,128,2048]{3,2,1,0:T(8,128)(2,1)S(1)} %dynamic-slice_bitcast_fusion.4), kind=kLoop, calls=%fused_computation.1.clone.1 | loop fusion | flops 5767168 | bytes 23068672 | tf_op jit(solution)/shard_map/while/body/eval_jaxpr/concatenate | solution.py:22
  327.2 9.9 %fusion.40 = (bf16[2,1408,1024]{2,1,0:T(8,128)(2,1)}, bf16[2,1408,1024]{2,1,0:T(8,128)(2,1)}) fusion(bf16[2,1408,2048]{2,1,0:T(8,128)(2,1)} %bitcast.72), kind=kLoop, calls=%fused_computation.38.clone.1 | loop fusion | bytes 23068672 | tf_op jit(solution)/shard_map/while/body/eval_jaxpr/slice | solution.py:24
  337.1 8.3 %copy.26 = bf16[2,1408,1024]{1,2,0:T(8,128)(2,1)} copy(bf16[2,1408,1024]{2,1,0:T(8,128)(2,1)} %get-tuple-element.170) | data formatting | bytes 11534336 | tf_op jit(solution)/shard_map/while/body/eval_jaxpr/slice | solution.py:24
  345.5 1.1 dynamic-slice_bitcast_fusion.5
  346.6 3.9 fusion.42
  350.5 4.2 copy-done.2
  354.7 2.4 fusion.43
  357.1 8.4 %copy.25 = bf16[2,1408,1024]{1,2,0:T(8,128)(2,1)} copy(bf16[2,1408,1024]{2,1,0:T(8,128)(2,1)} %get-tuple-element.169) | data formatting | bytes 11534336 | tf_op jit(solution)/shard_map/while/body/eval_jaxpr/slice | solution.py:25
  365.5 8.8 %divide_convert_fusion.2 = bf16[2,128,8,128]{1,3,2,0:T(8,128)(2,1)S(1)} fusion(bf16[2,1408,8,128]{1,3,2,0:T(8,128)(2,1)} %bitcast.76, f32[2,8,128,1408]{3,2,1,0:T(8,128)} %copy-done.2, f32[2,8,128]{2,1,0:T(8,128)S(1)} %get-tuple-element.172, pred[2,1408]{1,0:T(4,128)(4,1)S(1)} %broadcast_compare_fusion.2, f32[2,128,8]{1,2,0:T(8,128)S(1)} %bitcast.79), kind=kOutput, calls=%fused_computation.13.clone.1 | convolution fusion | flops 750256128 | bytes 17844992 | tf_op jit(solution)/shard_map/while/body/eval_jaxpr/bhqk,bkhd->bqhd/dot_general | solution.py:38
  374.9 0.8 constant_dynamic-update-slice_fusion.2
  376.8 1.3 dynamic-slice_bitcast_fusion.4
  378.2 0.7 compare_select_fusion.2
  378.9 10.0 %gather_fusion = bf16[20,128,2048]{2,1,0:T(8,128)(2,1)} fusion(bf16[24,128,2048]{2,1,0:T(8,128)(2,1)} %get-tuple-element.200, s32[1024]{0:T(1024)S(1)} %pad_clamp_fusion.2), kind=kCustom, calls=%fused_computation.clone.1 | custom fusion | bytes 20971600 | tf_op jit(solution)/shard_map/while/body/eval_jaxpr/gather | solution.py:73
  388.9 10.1 %pad_maximum_fusion.3 = bf16[2,11,128,2048]{3,2,1,0:T(8,128)(2,1)} fusion(bf16[2,10,128,2048]{3,2,1,0:T(8,128)(2,1)} %bitcast.74, bf16[2,1,128,2048]{3,2,1,0:T(8,128)(2,1)S(1)} %dynamic-slice_bitcast_fusion.4), kind=kLoop, calls=%fused_computation.1.clone.1 | loop fusion | flops 5767168 | bytes 23068672 | tf_op jit(solution)/shard_map/while/body/eval_jaxpr/concatenate | solution.py:22
  399.0 9.9 %fusion.40 = (bf16[2,1408,1024]{2,1,0:T(8,128)(2,1)}, bf16[2,1408,1024]{2,1,0:T(8,128)(2,1)}) fusion(bf16[2,1408,2048]{2,1,0:T(8,128)(2,1)} %bitcast.72), kind=kLoop, calls=%fused_computation.38.clone.1 | loop fusion | bytes 23068672 | tf_op jit(solution)/shard_map/while/body/eval_jaxpr/slice | solution.py:24
  408.9 8.3 %copy.26 = bf16[2,1408,1024]{1,2,0:T(8,128)(2,1)} copy(bf16[2,1408,1024]{2,1,0:T(8,128)(2,1)} %get-tuple-element.170) | data formatting | bytes 11534336 | tf_op jit(solution)/shard_map/while/body/eval_jaxpr/slice | solution.py:24
  417.3 1.1 dynamic-slice_bitcast_fusion.5
  418.5 3.9 fusion.42
  422.4 4.2 copy-done.2
  426.5 2.4 fusion.43
  428.9 8.4 %copy.25 = bf16[2,1408,1024]{1,2,0:T(8,128)(2,1)} copy(bf16[2,1408,1024]{2,1,0:T(8,128)(2,1)} %get-tuple-element.169) | data formatting | bytes 11534336 | tf_op jit(solution)/shard_map/while/body/eval_jaxpr/slice | solution.py:25
  437.3 8.8 %divide_convert_fusion.2 = bf16[2,128,8,128]{1,3,2,0:T(8,128)(2,1)S(1)} fusion(bf16[2,1408,8,128]{1,3,2,0:T(8,128)(2,1)} %bitcast.76, f32[2,8,128,1408]{3,2,1,0:T(8,128)} %copy-done.2, f32[2,8,128]{2,1,0:T(8,128)S(1)} %get-tuple-element.172, pred[2,1408]{1,0:T(4,128)(4,1)S(1)} %broadcast_compare_fusion.2, f32[2,128,8]{1,2,0:T(8,128)S(1)} %bitcast.79), kind=kOutput, calls=%fused_computation.13.clone.1 | convolution fusion | flops 750256128 | bytes 17844992 | tf_op jit(solution)/shard_map/while/body/eval_jaxpr/bhqk,bkhd->bqhd/dot_general | solution.py:38
  446.7 0.9 constant_dynamic-update-slice_fusion.2
  448.7 1.3 dynamic-slice_bitcast_fusion.4
  450.0 0.7 compare_select_fusion.2
  450.8 10.0 %gather_fusion = bf16[20,128,2048]{2,1,0:T(8,128)(2,1)} fusion(bf16[24,128,2048]{2,1,0:T(8,128)(2,1)} %get-tuple-element.200, s32[1024]{0:T(1024)S(1)} %pad_clamp_fusion.2), kind=kCustom, calls=%fused_computation.clone.1 | custom fusion | bytes 20971600 | tf_op jit(solution)/shard_map/while/body/eval_jaxpr/gather | solution.py:73
  460.8 10.1 %pad_maximum_fusion.3 = bf16[2,11,128,2048]{3,2,1,0:T(8,128)(2,1)} fusion(bf16[2,10,128,2048]{3,2,1,0:T(8,128)(2,1)} %bitcast.74, bf16[2,1,128,2048]{3,2,1,0:T(8,128)(2,1)S(1)} %dynamic-slice_bitcast_fusion.4), kind=kLoop, calls=%fused_computation.1.clone.1 | loop fusion | flops 5767168 | bytes 23068672 | tf_op jit(solution)/shard_map/while/body/eval_jaxpr/concatenate | solution.py:22
  470.8 9.9 %fusion.40 = (bf16[2,1408,1024]{2,1,0:T(8,128)(2,1)}, bf16[2,1408,1024]{2,1,0:T(8,128)(2,1)}) fusion(bf16[2,1408,2048]{2,1,0:T(8,128)(2,1)} %bitcast.72), kind=kLoop, calls=%fused_computation.38.clone.1 | loop fusion | bytes 23068672 | tf_op jit(solution)/shard_map/while/body/eval_jaxpr/slice | solution.py:24
  480.8 8.3 %copy.26 = bf16[2,1408,1024]{1,2,0:T(8,128)(2,1)} copy(bf16[2,1408,1024]{2,1,0:T(8,128)(2,1)} %get-tuple-element.170) | data formatting | bytes 11534336 | tf_op jit(solution)/shard_map/while/body/eval_jaxpr/slice | solution.py:24
  489.1 1.1 dynamic-slice_bitcast_fusion.5
  490.3 3.9 fusion.42
  494.2 4.2 copy-done.2
  498.4 2.4 fusion.43
  500.8 8.4 %copy.25 = bf16[2,1408,1024]{1,2,0:T(8,128)(2,1)} copy(bf16[2,1408,1024]{2,1,0:T(8,128)(2,1)} %get-tuple-element.169) | data formatting | bytes 11534336 | tf_op jit(solution)/shard_map/while/body/eval_jaxpr/slice | solution.py:25
  509.2 8.8 %divide_convert_fusion.2 = bf16[2,128,8,128]{1,3,2,0:T(8,128)(2,1)S(1)} fusion(bf16[2,1408,8,128]{1,3,2,0:T(8,128)(2,1)} %bitcast.76, f32[2,8,128,1408]{3,2,1,0:T(8,128)} %copy-done.2, f32[2,8,128]{2,1,0:T(8,128)S(1)} %get-tuple-element.172, pred[2,1408]{1,0:T(4,128)(4,1)S(1)} %broadcast_compare_fusion.2, f32[2,128,8]{1,2,0:T(8,128)S(1)} %bitcast.79), kind=kOutput, calls=%fused_computation.13.clone.1 | convolution fusion | flops 750256128 | bytes 17844992 | tf_op jit(solution)/shard_map/while/body/eval_jaxpr/bhqk,bkhd->bqhd/dot_general | solution.py:38
  518.5 0.8 constant_dynamic-update-slice_fusion.2
  520.5 1.3 dynamic-slice_bitcast_fusion.4
  521.8 0.7 compare_select_fusion.2
  522.6 10.0 %gather_fusion = bf16[20,128,2048]{2,1,0:T(8,128)(2,1)} fusion(bf16[24,128,2048]{2,1,0:T(8,128)(2,1)} %get-tuple-element.200, s32[1024]{0:T(1024)S(1)} %pad_clamp_fusion.2), kind=kCustom, calls=%fused_computation.clone.1 | custom fusion | bytes 20971600 | tf_op jit(solution)/shard_map/while/body/eval_jaxpr/gather | solution.py:73
  532.6 10.1 %pad_maximum_fusion.3 = bf16[2,11,128,2048]{3,2,1,0:T(8,128)(2,1)} fusion(bf16[2,10,128,2048]{3,2,1,0:T(8,128)(2,1)} %bitcast.74, bf16[2,1,128,2048]{3,2,1,0:T(8,128)(2,1)S(1)} %dynamic-slice_bitcast_fusion.4), kind=kLoop, calls=%fused_computation.1.clone.1 | loop fusion | flops 5767168 | bytes 23068672 | tf_op jit(solution)/shard_map/while/body/eval_jaxpr/concatenate | solution.py:22
  542.7 9.9 %fusion.40 = (bf16[2,1408,1024]{2,1,0:T(8,128)(2,1)}, bf16[2,1408,1024]{2,1,0:T(8,128)(2,1)}) fusion(bf16[2,1408,2048]{2,1,0:T(8,128)(2,1)} %bitcast.72), kind=kLoop, calls=%fused_computation.38.clone.1 | loop fusion | bytes 23068672 | tf_op jit(solution)/shard_map/while/body/eval_jaxpr/slice | solution.py:24
  552.6 8.3 %copy.26 = bf16[2,1408,1024]{1,2,0:T(8,128)(2,1)} copy(bf16[2,1408,1024]{2,1,0:T(8,128)(2,1)} %get-tuple-element.170) | data formatting | bytes 11534336 | tf_op jit(solution)/shard_map/while/body/eval_jaxpr/slice | solution.py:24
  561.0 1.1 dynamic-slice_bitcast_fusion.5
  562.1 3.9 fusion.42
  566.0 4.2 copy-done.2
  570.2 2.4 fusion.43
  572.6 8.4 %copy.25 = bf16[2,1408,1024]{1,2,0:T(8,128)(2,1)} copy(bf16[2,1408,1024]{2,1,0:T(8,128)(2,1)} %get-tuple-element.169) | data formatting | bytes 11534336 | tf_op jit(solution)/shard_map/while/body/eval_jaxpr/slice | solution.py:25
  581.0 8.8 %divide_convert_fusion.2 = bf16[2,128,8,128]{1,3,2,0:T(8,128)(2,1)S(1)} fusion(bf16[2,1408,8,128]{1,3,2,0:T(8,128)(2,1)} %bitcast.76, f32[2,8,128,1408]{3,2,1,0:T(8,128)} %copy-done.2, f32[2,8,128]{2,1,0:T(8,128)S(1)} %get-tuple-element.172, pred[2,1408]{1,0:T(4,128)(4,1)S(1)} %broadcast_compare_fusion.2, f32[2,128,8]{1,2,0:T(8,128)S(1)} %bitcast.79), kind=kOutput, calls=%fused_computation.13.clone.1 | convolution fusion | flops 750256128 | bytes 17844992 | tf_op jit(solution)/shard_map/while/body/eval_jaxpr/bhqk,bkhd->bqhd/dot_general | solution.py:38
  590.4 0.8 constant_dynamic-update-slice_fusion.2
  591.2 6.0 convolution_convert_fusion.1
  (55 shorter events, 5.6 us)
Async XLA Ops:
  6.5 135.1 %copy-start = (bf16[1024,1024]{1,0:T(8,128)(2,1)S(1)}, bf16[1024,1024]{1,0:T(8,128)(2,1)}, u32[]{:S(2)}) copy-start(bf16[1024,1024]{1,0:T(8,128)(2,1)} %param.7) | copy-start | bytes 6291460
  6.5 135.1 %all-gather.3.cloned.1.call-start = ((), (), s32[]{:S(2)}) async-start(), calls=%async_computation | async-start | bytes 7077888 | tf_op jit(solution)/shard_map/all_gather | solution.py:53
  7.3 583.9 %all-gather.5.cloned.1.call-start = ((), (), s32[]{:S(2)}) async-start(), calls=%async_computation.1 | async-start | bytes 2359296 | tf_op jit(solution)/shard_map/all_gather | solution.py:88
  151.3 2.7 copy-start.3
  153.9 5.5 copy-start.4
  156.2 133.3 %collective-permute-start = (bf16[1024,2048]{1,0:T(8,128)(2,1)}, bf16[1024,2048]{1,0:T(8,128)(2,1)}, u32[]{:S(2)}, u32[]{:S(2)}) collective-permute-start(bf16[1024,2048]{1,0:T(8,128)(2,1)} %slice.24), channel_id=1, source_target_pairs={{0,8},{8,16},{16,24},{24,32},{32,40},{40,48},{48,56},{56,64},{64,7... | collective-permute-start | bytes 12582920 | tf_op jit(solution)/shard_map/ppermute | solution.py:15
  159.4 133.1 %collective-permute-start.1 = (bf16[1024,2048]{1,0:T(8,128)(2,1)}, bf16[1024,2048]{1,0:T(8,128)(2,1)}, u32[]{:S(2)}, u32[]{:S(2)}) collective-permute-start(bf16[1024,2048]{1,0:T(8,128)(2,1)} %slice.24), channel_id=1, source_target_pairs={{0,120},{8,0},{16,8},{24,16},{32,24},{40,32},{48,40},{56,48},{64,5... | collective-permute-start | bytes 12582920 | tf_op jit(solution)/shard_map/ppermute | solution.py:15
  350.5 4.2 copy-start.2
  422.3 4.2 copy-start.2
  494.2 4.2 copy-start.2
  566.0 4.2 copy-start.2
  591.2 6.0 copy-start.1
Sparse Core Ops, SparseCore 0:
  9.0 132.5 all-gather.2
  159.5 109.6 all-gather.4
where the time goes:
time: 607 us; the launch traced here: 604 us
  waiting for transfers between devices  265 us (44%)
  local copies, waits for them, and re-layouts  189 us (31%)
  matrix products  66.5 us (11%)
  other arithmetic  64.4 us (11%)
  between operations  13.4 us (2%)
    all_gather x1, waiting for transfers between devices, shards(): lax.all_gather(w_qkv, 'fsdp', axis=0, tiled=True)  134 us
    ppermute x2, waiting for transfers between devices, from_behind(): return lax.ppermute(value, axis, pairs)  130 us
    slice x8, local copies, waits for them, and re-layouts, attend(): keyvals[..., :feature_width].reshape(block_count, -1, HEADS, head_width)  72.8 us
    concatenate x4, other arithmetic, attend(): keyvals = jnp.concatenate([own_blocks[:, None], picked], axis=1)  40.2 us
    gather x4, local copies, waits for them, and re-layouts, one_group(): picked = pool[layout_part]  40 us
    dot_general x4, matrix products, attend(): jnp.einsum('bhqk,bkhd->bqhd', rounded, value_heads, preferred_element_typ...  35.3 us
    slice x4, local copies, waits for them, and re-layouts, attend(): keyvals[..., feature_width:].reshape(block_count, -1, HEADS, head_width)  33.5 us
    while x16, local copies, waits for them, and re-layouts  21.4 us
  transfers between devices with their start and end apart: 4, of which 3 were waited for; matrix products, arithmetic and copies ran while one was open for 47% of the time, Pallas kernels for 0%

commit v1 on v0

--- a/solution.py
+++ b/solution.py
@@ -50,7 +50,9 @@
     fresh = [
         jnp.dot(
             own_cols,
-            lax.all_gather(w_qkv, "fsdp", axis=0, tiled=True),
+            jnp.concatenate(
+                lax.all_to_all(jnp.stack([w_qkv] * lax.axis_size("fsdp")), "fsdp", 0, 0), axis=0
+            ),
             preferred_element_type=jnp.float32,
         )
     ]

time: 607 us -> 551 us (0.908)
  waiting for transfers between devices: 265 us -> 130 us
  blocking collectives: 0 us -> 78.7 us
    all_gather x1 -> x0, waiting for transfers between devices: 134 us -> none  [shards(): lax.all_gather(w_qkv, 'fsdp', axis=0, tiled=True)]
    all_to_all x0 -> x1, blocking collectives: none -> 78.7 us  [shards(): lax.all_to_all(jnp.stack([w_qkv] * lax.axis_size('fsdp')), 'fsdp', 0, 0)]
  transfers between devices with their start and end apart: 4 -> 3, of which waited for: 3 -> 2; matrix products, arithmetic and copies ran while one was open for 47% -> 52% of each run, Pallas kernels for 0% -> 0%
where the time goes in v1:
time: 551 us; the launch traced here: 549 us
  local copies, waits for them, and re-layouts  191 us (35%)
  waiting for transfers between devices  130 us (24%)
  blocking collectives  78.7 us (14%)
  other arithmetic  64.4 us (12%)
  matrix products  63.9 us (12%)
  between operations  13.4 us (2%)
    ppermute x2, waiting for transfers between devices, from_behind(): return lax.ppermute(value, axis, pairs)  130 us
    all_to_all x1, blocking collectives, shards(): lax.all_to_all(jnp.stack([w_qkv] * lax.axis_size('fsdp')), 'fsdp', 0, 0)  78.7 us
    slice x8, local copies, waits for them, and re-layouts, attend(): keyvals[..., :feature_width].reshape(block_count, -1, HEADS, head_width)  72.8 us
    concatenate x4, other arithmetic, attend(): keyvals = jnp.concatenate([own_blocks[:, None], picked], axis=1)  40.3 us
    gather x4, local copies, waits for them, and re-layouts, one_group(): picked = pool[layout_part]  39.9 us
    dot_general x4, matrix products, attend(): jnp.einsum('bhqk,bkhd->bqhd', rounded, value_heads, preferred_element_typ...  35.3 us
    slice x4, local copies, waits for them, and re-layouts, attend(): keyvals[..., feature_width:].reshape(block_count, -1, HEADS, head_width)  33.4 us
    while x16, local copies, waits for them, and re-layouts  21.4 us
  transfers between devices with their start and end apart: 3, of which 2 were waited for; matrix products, arithmetic and copies ran while one was open for 52% of the time, Pallas kernels for 0%

profile of v1, /device:TPU:1, one launch (start us, length us, event | category | flops | bytes accessed | tf_op | source)
XLA Modules:
  0.0 548.6 jit_solution(1069191660410699090)
XLA Ops:
  6.5 2.1 stack.2
  8.6 78.7 %all_to_all.5 = bf16[8,128,3072]{2,1,0:T(8,128)(2,1)S(1)} all-to-all(bf16[8,128,3072]{2,1,0:T(8,128)(2,1)S(1)} %stack.2), channel_id=1, replica_groups=mesh['seq'=16,'fsdp'=8] {'fsdp'}, dimensions={0} | all-to-all | bytes 12582912 | tf_op jit(solution)/shard_map/all_to_all | solution.py:54
  87.3 7.1 %convolution_convert_fusion = bf16[1024,3072]{1,0:T(8,128)(2,1)S(1)} fusion(bf16[1024,1024]{1,0:T(8,128)(2,1)S(1)} %copy-done, bf16[1024,3072]{1,0:T(8,128)(2,1)S(1)} %bitcast.80), kind=kOutput, calls=%fused_computation.36 | convolution fusion | flops 6445596672 | bytes 14680064 | tf_op jit(solution)/shard_map/dot_general | solution.py:51
  94.4 2.6 copy-done.3
  97.0 2.2 slice.24
  99.3 4.4 collective-permute-start
  103.8 3.1 slice.25
  106.9 126.8 %collective-permute-done = bf16[1024,2048]{1,0:T(8,128)(2,1)} collective-permute-done((bf16[1024,2048]{1,0:T(8,128)(2,1)}, bf16[1024,2048]{1,0:T(8,128)(2,1)}, u32[]{:S(2)}, u32[]{:S(2)}) %collective-permute-start) | collective-permute-done | bytes 4194336 | tf_op jit(solution)/shard_map/ppermute | solution.py:15
  233.7 2.9 collective-permute-done.1
  236.6 11.3 %pad_maximum_fusion.1 = bf16[3072,2048]{1,0:T(8,128)(2,1)} fusion(bf16[1024,2048]{1,0:T(8,128)(2,1)} %collective-permute-done.1, bf16[1024,2048]{1,0:T(8,128)(2,1)} %slice.24, bf16[1024,2048]{1,0:T(8,128)(2,1)} %collective-permute-done), kind=kLoop, calls=%fused_computation.35 | loop fusion | flops 37748736 | bytes 25165824 | tf_op jit(solution)/shard_map/concatenate | solution.py:65
  247.9 287.8 %while.12 = (s32[]{:T(128)}, bf16[4,256,1024]{2,1,0:T(8,128)(2,1)}, s32[4]{0:T(128)S(1)}, bf16[24,128,2048]{2,1,0:T(8,128)(2,1)}, s32[4,2,10]{2,1,0:T(2,128)}, /...) while((s32[]{:T(128)}, bf16[4,256,1024]{2,1,0:T(8,128)(2,1)}, ...), condition=%wide.region_3.4_spmd, body=%wide.region_0.3_spmd.sunk | while | flops 1514416896 | bytes 190909680 | solution.py:78
  249.2 1.3 dynamic-slice_bitcast_fusion.4
  250.5 0.7 compare_select_fusion.2
  251.3 10.0 %gather_fusion = bf16[20,128,2048]{2,1,0:T(8,128)(2,1)} fusion(bf16[24,128,2048]{2,1,0:T(8,128)(2,1)} %get-tuple-element.200, s32[1024]{0:T(1024)S(1)} %pad_clamp_fusion.2), kind=kCustom, calls=%fused_computation.clone.1 | custom fusion | bytes 20971600 | tf_op jit(solution)/shard_map/while/body/eval_jaxpr/gather | solution.py:75
  261.3 10.1 %pad_maximum_fusion.3 = bf16[2,11,128,2048]{3,2,1,0:T(8,128)(2,1)} fusion(bf16[2,10,128,2048]{3,2,1,0:T(8,128)(2,1)} %bitcast.75, bf16[2,1,128,2048]{3,2,1,0:T(8,128)(2,1)S(1)} %dynamic-slice_bitcast_fusion.4), kind=kLoop, calls=%fused_computation.1.clone.1 | loop fusion | flops 5767168 | bytes 23068672 | tf_op jit(solution)/shard_map/while/body/eval_jaxpr/concatenate | solution.py:22
  271.3 9.9 %fusion.40 = (bf16[2,1408,1024]{2,1,0:T(8,128)(2,1)}, bf16[2,1408,1024]{2,1,0:T(8,128)(2,1)}) fusion(bf16[2,1408,2048]{2,1,0:T(8,128)(2,1)} %bitcast.73), kind=kLoop, calls=%fused_computation.38.clone.1 | loop fusion | bytes 23068672 | tf_op jit(solution)/shard_map/while/body/eval_jaxpr/slice | solution.py:24
  281.3 8.3 %copy.26 = bf16[2,1408,1024]{1,2,0:T(8,128)(2,1)} copy(bf16[2,1408,1024]{2,1,0:T(8,128)(2,1)} %get-tuple-element.170) | data formatting | bytes 11534336 | tf_op jit(solution)/shard_map/while/body/eval_jaxpr/slice | solution.py:24
  289.6 1.1 dynamic-slice_bitcast_fusion.5
  290.8 3.9 fusion.42
  294.7 4.2 copy-done.2
  298.9 2.4 fusion.43
  301.3 8.4 %copy.25 = bf16[2,1408,1024]{1,2,0:T(8,128)(2,1)} copy(bf16[2,1408,1024]{2,1,0:T(8,128)(2,1)} %get-tuple-element.169) | data formatting | bytes 11534336 | tf_op jit(solution)/shard_map/while/body/eval_jaxpr/slice | solution.py:25
  309.7 8.8 %divide_convert_fusion.2 = bf16[2,128,8,128]{1,3,2,0:T(8,128)(2,1)S(1)} fusion(bf16[2,1408,8,128]{1,3,2,0:T(8,128)(2,1)} %bitcast.77, f32[2,8,128,1408]{3,2,1,0:T(8,128)} %copy-done.2, f32[2,8,128]{2,1,0:T(8,128)S(1)} %get-tuple-element.172, pred[2,1408]{1,0:T(4,128)(4,1)S(1)} %broadcast_compare_fusion.2, f32[2,128,8]{1,2,0:T(8,128)S(1)} %bitcast.81), kind=kOutput, calls=%fused_computation.13.clone.1 | convolution fusion | flops 750256128 | bytes 17844992 | tf_op jit(solution)/shard_map/while/body/eval_jaxpr/bhqk,bkhd->bqhd/dot_general | solution.py:38
  319.0 0.8 constant_dynamic-update-slice_fusion.2
  321.1 1.3 dynamic-slice_bitcast_fusion.4
  322.5 0.7 compare_select_fusion.2
  323.2 10.0 %gather_fusion = bf16[20,128,2048]{2,1,0:T(8,128)(2,1)} fusion(bf16[24,128,2048]{2,1,0:T(8,128)(2,1)} %get-tuple-element.200, s32[1024]{0:T(1024)S(1)} %pad_clamp_fusion.2), kind=kCustom, calls=%fused_computation.clone.1 | custom fusion | bytes 20971600 | tf_op jit(solution)/shard_map/while/body/eval_jaxpr/gather | solution.py:75
  333.2 10.1 %pad_maximum_fusion.3 = bf16[2,11,128,2048]{3,2,1,0:T(8,128)(2,1)} fusion(bf16[2,10,128,2048]{3,2,1,0:T(8,128)(2,1)} %bitcast.75, bf16[2,1,128,2048]{3,2,1,0:T(8,128)(2,1)S(1)} %dynamic-slice_bitcast_fusion.4), kind=kLoop, calls=%fused_computation.1.clone.1 | loop fusion | flops 5767168 | bytes 23068672 | tf_op jit(solution)/shard_map/while/body/eval_jaxpr/concatenate | solution.py:22
  343.3 9.9 %fusion.40 = (bf16[2,1408,1024]{2,1,0:T(8,128)(2,1)}, bf16[2,1408,1024]{2,1,0:T(8,128)(2,1)}) fusion(bf16[2,1408,2048]{2,1,0:T(8,128)(2,1)} %bitcast.73), kind=kLoop, calls=%fused_computation.38.clone.1 | loop fusion | bytes 23068672 | tf_op jit(solution)/shard_map/while/body/eval_jaxpr/slice | solution.py:24
  353.2 8.3 %copy.26 = bf16[2,1408,1024]{1,2,0:T(8,128)(2,1)} copy(bf16[2,1408,1024]{2,1,0:T(8,128)(2,1)} %get-tuple-element.170) | data formatting | bytes 11534336 | tf_op jit(solution)/shard_map/while/body/eval_jaxpr/slice | solution.py:24
  361.6 1.1 dynamic-slice_bitcast_fusion.5
  362.8 3.9 fusion.42
  366.6 4.2 copy-done.2
  370.8 2.4 fusion.43
  373.3 8.4 %copy.25 = bf16[2,1408,1024]{1,2,0:T(8,128)(2,1)} copy(bf16[2,1408,1024]{2,1,0:T(8,128)(2,1)} %get-tuple-element.169) | data formatting | bytes 11534336 | tf_op jit(solution)/shard_map/while/body/eval_jaxpr/slice | solution.py:25
  381.6 8.8 %divide_convert_fusion.2 = bf16[2,128,8,128]{1,3,2,0:T(8,128)(2,1)S(1)} fusion(bf16[2,1408,8,128]{1,3,2,0:T(8,128)(2,1)} %bitcast.77, f32[2,8,128,1408]{3,2,1,0:T(8,128)} %copy-done.2, f32[2,8,128]{2,1,0:T(8,128)S(1)} %get-tuple-element.172, pred[2,1408]{1,0:T(4,128)(4,1)S(1)} %broadcast_compare_fusion.2, f32[2,128,8]{1,2,0:T(8,128)S(1)} %bitcast.81), kind=kOutput, calls=%fused_computation.13.clone.1 | convolution fusion | flops 750256128 | bytes 17844992 | tf_op jit(solution)/shard_map/while/body/eval_jaxpr/bhqk,bkhd->bqhd/dot_general | solution.py:38
  391.0 0.9 constant_dynamic-update-slice_fusion.2
  393.1 1.3 dynamic-slice_bitcast_fusion.4
  394.4 0.7 compare_select_fusion.2
  395.2 10.0 %gather_fusion = bf16[20,128,2048]{2,1,0:T(8,128)(2,1)} fusion(bf16[24,128,2048]{2,1,0:T(8,128)(2,1)} %get-tuple-element.200, s32[1024]{0:T(1024)S(1)} %pad_clamp_fusion.2), kind=kCustom, calls=%fused_computation.clone.1 | custom fusion | bytes 20971600 | tf_op jit(solution)/shard_map/while/body/eval_jaxpr/gather | solution.py:75
  405.2 10.1 %pad_maximum_fusion.3 = bf16[2,11,128,2048]{3,2,1,0:T(8,128)(2,1)} fusion(bf16[2,10,128,2048]{3,2,1,0:T(8,128)(2,1)} %bitcast.75, bf16[2,1,128,2048]{3,2,1,0:T(8,128)(2,1)S(1)} %dynamic-slice_bitcast_fusion.4), kind=kLoop, calls=%fused_computation.1.clone.1 | loop fusion | flops 5767168 | bytes 23068672 | tf_op jit(solution)/shard_map/while/body/eval_jaxpr/concatenate | solution.py:22
  415.3 9.9 %fusion.40 = (bf16[2,1408,1024]{2,1,0:T(8,128)(2,1)}, bf16[2,1408,1024]{2,1,0:T(8,128)(2,1)}) fusion(bf16[2,1408,2048]{2,1,0:T(8,128)(2,1)} %bitcast.73), kind=kLoop, calls=%fused_computation.38.clone.1 | loop fusion | bytes 23068672 | tf_op jit(solution)/shard_map/while/body/eval_jaxpr/slice | solution.py:24
  425.2 8.3 %copy.26 = bf16[2,1408,1024]{1,2,0:T(8,128)(2,1)} copy(bf16[2,1408,1024]{2,1,0:T(8,128)(2,1)} %get-tuple-element.170) | data formatting | bytes 11534336 | tf_op jit(solution)/shard_map/while/body/eval_jaxpr/slice | solution.py:24
  433.5 1.1 dynamic-slice_bitcast_fusion.5
  434.7 3.9 fusion.42
  438.6 4.2 copy-done.2
  442.8 2.4 fusion.43
  445.2 8.4 %copy.25 = bf16[2,1408,1024]{1,2,0:T(8,128)(2,1)} copy(bf16[2,1408,1024]{2,1,0:T(8,128)(2,1)} %get-tuple-element.169) | data formatting | bytes 11534336 | tf_op jit(solution)/shard_map/while/body/eval_jaxpr/slice | solution.py:25
  453.6 8.8 %divide_convert_fusion.2 = bf16[2,128,8,128]{1,3,2,0:T(8,128)(2,1)S(1)} fusion(bf16[2,1408,8,128]{1,3,2,0:T(8,128)(2,1)} %bitcast.77, f32[2,8,128,1408]{3,2,1,0:T(8,128)} %copy-done.2, f32[2,8,128]{2,1,0:T(8,128)S(1)} %get-tuple-element.172, pred[2,1408]{1,0:T(4,128)(4,1)S(1)} %broadcast_compare_fusion.2, f32[2,128,8]{1,2,0:T(8,128)S(1)} %bitcast.81), kind=kOutput, calls=%fused_computation.13.clone.1 | convolution fusion | flops 750256128 | bytes 17844992 | tf_op jit(solution)/shard_map/while/body/eval_jaxpr/bhqk,bkhd->bqhd/dot_general | solution.py:38
  462.9 0.8 constant_dynamic-update-slice_fusion.2
  465.0 1.3 dynamic-slice_bitcast_fusion.4
  466.4 0.7 compare_select_fusion.2
  467.1 10.0 %gather_fusion = bf16[20,128,2048]{2,1,0:T(8,128)(2,1)} fusion(bf16[24,128,2048]{2,1,0:T(8,128)(2,1)} %get-tuple-element.200, s32[1024]{0:T(1024)S(1)} %pad_clamp_fusion.2), kind=kCustom, calls=%fused_computation.clone.1 | custom fusion | bytes 20971600 | tf_op jit(solution)/shard_map/while/body/eval_jaxpr/gather | solution.py:75
  477.1 10.1 %pad_maximum_fusion.3 = bf16[2,11,128,2048]{3,2,1,0:T(8,128)(2,1)} fusion(bf16[2,10,128,2048]{3,2,1,0:T(8,128)(2,1)} %bitcast.75, bf16[2,1,128,2048]{3,2,1,0:T(8,128)(2,1)S(1)} %dynamic-slice_bitcast_fusion.4), kind=kLoop, calls=%fused_computation.1.clone.1 | loop fusion | flops 5767168 | bytes 23068672 | tf_op jit(solution)/shard_map/while/body/eval_jaxpr/concatenate | solution.py:22
  487.2 9.9 %fusion.40 = (bf16[2,1408,1024]{2,1,0:T(8,128)(2,1)}, bf16[2,1408,1024]{2,1,0:T(8,128)(2,1)}) fusion(bf16[2,1408,2048]{2,1,0:T(8,128)(2,1)} %bitcast.73), kind=kLoop, calls=%fused_computation.38.clone.1 | loop fusion | bytes 23068672 | tf_op jit(solution)/shard_map/while/body/eval_jaxpr/slice | solution.py:24
  497.1 8.3 %copy.26 = bf16[2,1408,1024]{1,2,0:T(8,128)(2,1)} copy(bf16[2,1408,1024]{2,1,0:T(8,128)(2,1)} %get-tuple-element.170) | data formatting | bytes 11534336 | tf_op jit(solution)/shard_map/while/body/eval_jaxpr/slice | solution.py:24
  505.5 1.1 dynamic-slice_bitcast_fusion.5
  506.7 3.9 fusion.42
  510.6 4.2 copy-done.2
  514.7 2.4 fusion.43
  517.2 8.4 %copy.25 = bf16[2,1408,1024]{1,2,0:T(8,128)(2,1)} copy(bf16[2,1408,1024]{2,1,0:T(8,128)(2,1)} %get-tuple-element.169) | data formatting | bytes 11534336 | tf_op jit(solution)/shard_map/while/body/eval_jaxpr/slice | solution.py:25
  525.5 8.8 %divide_convert_fusion.2 = bf16[2,128,8,128]{1,3,2,0:T(8,128)(2,1)S(1)} fusion(bf16[2,1408,8,128]{1,3,2,0:T(8,128)(2,1)} %bitcast.77, f32[2,8,128,1408]{3,2,1,0:T(8,128)} %copy-done.2, f32[2,8,128]{2,1,0:T(8,128)S(1)} %get-tuple-element.172, pred[2,1408]{1,0:T(4,128)(4,1)S(1)} %broadcast_compare_fusion.2, f32[2,128,8]{1,2,0:T(8,128)S(1)} %bitcast.81), kind=kOutput, calls=%fused_computation.13.clone.1 | convolution fusion | flops 750256128 | bytes 17844992 | tf_op jit(solution)/shard_map/while/body/eval_jaxpr/bhqk,bkhd->bqhd/dot_general | solution.py:38
  534.9 0.8 constant_dynamic-update-slice_fusion.2
  535.7 6.0 %convolution_convert_fusion.1 = bf16[1024,1024]{1,0:T(8,128)(2,1)} fusion(bf16[1024,1024]{1,0:T(8,128)(2,1)} %bitcast.83, bf16[1024,1024]{1,0:T(8,128)(2,1)} %all-gather.2.cloned.1.call-done), kind=kOutput, calls=%fused_computation.37 | convolution fusion | flops 2148532224 | bytes 6291456 | tf_op jit(solution)/shard_map/dot_general | solution.py:88
  (54 shorter events, 5.8 us)
Async XLA Ops:
  6.5 80.7 %copy-start = (bf16[1024,1024]{1,0:T(8,128)(2,1)S(1)}, bf16[1024,1024]{1,0:T(8,128)(2,1)}, u32[]{:S(2)}) copy-start(bf16[1024,1024]{1,0:T(8,128)(2,1)} %param.7) | copy-start | bytes 6291460
  6.5 529.2 %all-gather.2.cloned.1.call-start = ((), (), s32[]{:S(2)}) async-start(), calls=%async_computation.1 | async-start | bytes 2359296 | tf_op jit(solution)/shard_map/all_gather | solution.py:90
  94.4 2.7 copy-start.3
  97.0 6.7 %copy-start.4 = (s32[8]{0:T(128)S(1)}, s32[8]{0:T(128)}, u32[]{:S(2)}) copy-start(s32[8]{0:T(128)} %param.11) | copy-start | bytes 100
  99.3 134.4 %collective-permute-start = (bf16[1024,2048]{1,0:T(8,128)(2,1)}, bf16[1024,2048]{1,0:T(8,128)(2,1)}, u32[]{:S(2)}, u32[]{:S(2)}) collective-permute-start(bf16[1024,2048]{1,0:T(8,128)(2,1)} %slice.24), channel_id=1, source_target_pairs={{0,8},{8,16},{16,24},{24,32},{32,40},{40,48},{48,56},{56,64},{64,7... | collective-permute-start | bytes 12582920 | tf_op jit(solution)/shard_map/ppermute | solution.py:15
  103.7 132.9 %collective-permute-start.1 = (bf16[1024,2048]{1,0:T(8,128)(2,1)}, bf16[1024,2048]{1,0:T(8,128)(2,1)}, u32[]{:S(2)}, u32[]{:S(2)}) collective-permute-start(bf16[1024,2048]{1,0:T(8,128)(2,1)} %slice.24), channel_id=1, source_target_pairs={{0,120},{8,0},{16,8},{24,16},{32,24},{40,32},{48,40},{56,48},{64,5... | collective-permute-start | bytes 12582920 | tf_op jit(solution)/shard_map/ppermute | solution.py:15
  294.7 4.2 copy-start.2
  366.6 4.2 copy-start.2
  438.6 4.2 copy-start.2
  510.6 4.2 copy-start.2
  535.7 6.0 %copy-start.1 = (bf16[1024,1024]{1,0:T(8,128)(2,1)S(1)}, bf16[1024,1024]{1,0:T(8,128)(2,1)}, u32[]{:S(2)}) copy-start(bf16[1024,1024]{1,0:T(8,128)(2,1)} %param.7) | copy-start | bytes 6291460
Sparse Core Ops, SparseCore 0:
  103.8 108.8 all-gather.1
